TPU v7x, 512 devices: a whole 4x4x16 slice. The times are simulated.
512 devices in a mesh: gx: 32 (over y_lo, z), gy: 16 (over x, y_hi, core).
Axes of the slice: x: 4, y: 4 (y_hi: 2, y_lo: 2; y = y_hi * 2 + y_lo), z: 16, core: 2. Of those that a mesh axis runs over, the one named last changes fastest.
Arguments:
- mass_per_volume: float32 [256, 512, 128], P('gx', 'gy'), may hold values from 0.5 to 2
- momentum: float32 [3, 256, 512, 128], P(None, 'gx', 'gy'), may hold values from -0.9 to 0.9
- energy: float32 [256, 512, 128], P('gx', 'gy'), may hold values from 3 to 8
Outputs:
- tendency: float32 [5, 256, 512, 128], P(None, 'gx', 'gy')
- advanced: float32 [5, 256, 512, 128], P(None, 'gx', 'gy')
All inputs are finite; a program needn't handle non-finite values.
Results may differ from a plain program's by a relative error of at most 0.00016.
Values sent between devices are 32-bit elements; how exact they have to be, the bound alone decides.
A program may use at most 64 MiB of HBM per device.

v0:
```python
import jax
import jax.numpy as jnp
import numpy as np
from jax import lax
from jax.sharding import PartitionSpec as P

CX = 8
CY = 8
NZ = 512
HALO = 4
heat_ratio = 1.4
shear_resistance_reference = 0.08
sutherland_power_law = 0.7
prandtl = 0.72
section_step = 0.05
compact_alpha = 1.0 / 3.0
compact_near = 14.0 / 9.0
compact_far = 1.0 / 9.0


def padded(array, sides, width):
    for axis, dim in sides:
        devices, length = (lax.axis_size(axis), array.shape[dim])
        up = [(i, (i + 1) % devices) for i in range(devices)]
        down = [(j, i) for i, j in up]
        last = lax.slice_in_dim(array, length - width, length, axis=dim)
        initial = lax.slice_in_dim(array, 0, width, axis=dim)
        before = lax.ppermute(last, axis, up)
        after = lax.ppermute(initial, axis, down)
        array = jnp.concatenate([before, array, after], axis=dim)
    return array


def tridiagonal_inverse_product(length, stencil):
    solved = np.array(stencil)
    upper_ratio = np.zeros(length)
    for row_index in range(length):
        if row_index == 0:
            pivot_value = 1.0
            solved[row_index] = solved[row_index] / pivot_value
        else:
            pivot_value = 1.0 - compact_alpha * upper_ratio[row_index - 1]
            solved[row_index] = (
                solved[row_index] - compact_alpha * solved[row_index - 1]
            ) / pivot_value
        upper_ratio[row_index] = compact_alpha / pivot_value
    for row_index in range(length - 2, -1, -1):
        solved[row_index] = solved[row_index] - upper_ratio[row_index] * solved[row_index + 1]
    return solved


def compact_matrix(block_size, margin):
    length = block_size + 2 * margin
    stencil = compact_near / 2.0 * (np.eye(length, k=1) - np.eye(length, k=-1))
    stencil = stencil + compact_far / 4.0 * (np.eye(length, k=2) - np.eye(length, k=-2))
    inverse_product = tridiagonal_inverse_product(length, stencil)
    return inverse_product[margin : margin + block_size].astype(np.float32)


def pitch_matrix(total, block_size):
    matrix = compact_matrix(block_size, HALO)
    result = np.zeros((total, total), np.float32)
    rows_all = np.arange(total)
    block_start = rows_all // block_size * block_size
    for offset in range(block_size + 2 * HALO):
        columns = (block_start - HALO + offset) % total
        result[rows_all, columns] += matrix[rows_all % block_size, offset]
    return result


def span_matrix(total):
    offsets = np.arange(total)[:, None] - np.arange(total)[None, :]
    angles = np.pi * offsets / total
    signs = np.where(offsets % 2 == 0, 1.0, -1.0)
    sines = np.where(offsets == 0, 1.0, np.sin(angles))
    result = np.where(offsets == 0, 0.0, np.pi / total * signs * np.cos(angles) / sines)
    return result.astype(np.float32)


def right_side(conserved, gradients_of, derive_x, derive_y, derive_z):
    mass_per_volume = conserved[0]
    momentum = conserved[1:4]
    energy = conserved[4]
    local_speed_vector = momentum / mass_per_volume
    kinetic = 0.5 * jnp.sum(momentum * local_speed_vector, axis=0)
    normal_force_per_area = (heat_ratio - 1.0) * (energy - kinetic)
    thermal_state = normal_force_per_area / mass_per_volume
    basic_quantities = jnp.concatenate([local_speed_vector, thermal_state[None]], 0)
    gradients = gradients_of(basic_quantities)
    shear_resistance = shear_resistance_reference * jnp.power(thermal_state, sutherland_power_law)
    conductivity = shear_resistance * heat_ratio / ((heat_ratio - 1.0) * prandtl)
    dilatation = gradients[0][0] + gradients[1][1] + gradients[2][2]
    derivers = (derive_x, derive_y, derive_z)
    accumulated = None
    for direction in range(3):
        stress_column = [
            shear_resistance * (gradients[direction][component] + gradients[component][direction])
            for component in range(3)
        ]
        stress_column[direction] = (
            stress_column[direction] - 2.0 / 3.0 * shear_resistance * dilatation
        )
        fluxes = [momentum[direction]]
        for component in range(3):
            moment_flux = (
                momentum[component] * local_speed_vector[direction] - stress_column[component]
            )
            if component == direction:
                moment_flux = moment_flux + normal_force_per_area
            fluxes.append(moment_flux)
        work_term = (
            stress_column[0] * local_speed_vector[0]
            + stress_column[1] * local_speed_vector[1]
            + stress_column[2] * local_speed_vector[2]
        )
        fluxes.append(
            (energy + normal_force_per_area) * local_speed_vector[direction]
            - work_term
            - conductivity * gradients[direction][3]
        )
        divergence_part = derivers[direction](jnp.stack(fluxes))
        accumulated = divergence_part if accumulated is None else accumulated + divergence_part
    return -accumulated


def per_device(mass_per_volume, momentum, energy):
    conserved = jnp.concatenate([mass_per_volume[None], momentum, energy[None]], 0)
    highest = lax.Precision.HIGHEST
    x_matrix = jnp.asarray(compact_matrix(CX, HALO))
    z_matrix = jnp.asarray(span_matrix(NZ))

    def apply_x(extended):
        return jnp.einsum("il,flab->fiab", x_matrix, extended, precision=highest)

    def flux_x(values):
        return apply_x(padded(values, (("gx", 1),), HALO))

    y_matrix = jnp.asarray(pitch_matrix(conserved.shape[3], CY))

    def apply_y(values):
        return jnp.einsum("fabk,jk->fabj", values, y_matrix, precision=highest)

    def derive_span(values):
        lines = jnp.transpose(
            lax.all_to_all(values, "gy", split_axis=3, concat_axis=2, tiled=True), (0, 1, 3, 2)
        )
        derived = jnp.einsum("fack,jk->facj", lines, z_matrix, precision=highest)
        returned = lax.all_to_all(derived, "gy", split_axis=3, concat_axis=2, tiled=True)
        return jnp.transpose(returned, (0, 1, 3, 2))

    def gradients_of(basic_quantities):
        extended = padded(basic_quantities, (("gx", 1),), HALO)
        return (apply_x(extended), apply_y(basic_quantities), derive_span(basic_quantities))

    tendency = right_side(conserved, gradients_of, flux_x, apply_y, derive_span)
    advanced = conserved + section_step * tendency
    return (tendency, advanced)


def solution(mesh):
    in_specs = (P("gx", "gy", None), P(None, "gx", "gy", None), P("gx", "gy", None))
    out_specs = (P(None, "gx", "gy", None), P(None, "gx", "gy", None))
    return jax.shard_map(
        per_device, mesh=mesh, in_specs=in_specs, out_specs=out_specs, check_vma=False
    )
```

profile of v0, /device:TPU:7, one launch (start us, length us, event | category | flops | bytes accessed | tf_op | source)
XLA Modules:
  0.0 198.3 jit_solution(11590446967682339407)
XLA Ops:
  5.6 2.9 %copy.103 = f32[4,8,32,128]{2,1,0,3:T(8,128)S(1)} copy(f32[4,8,32,128]{3,1,2,0:T(8,128)} %pad_maximum_fusion) | data formatting | bytes 1048576 | tf_op jit(solution)/shard_map/concatenate | solution.py:88
  10.2 9.6 %all-to-all-start = ((f32[16,1,8192]{2,1,0:T(1,128)}), f32[16,1,8192]{2,1,0:T(1,128)S(1)}, u32[]{:S(2)}, u32[]{:S(2)}) async-start(f32[16,1,8192]{2,1,0:T(1,128)} %reshape.16), calls=%async_computation | async-start | bytes 1048576 | tf_op jit(solution)/shard_map/all_to_all | solution.py:145
  22.5 9.4 %collective-permute-start.1 = (f32[4,4,32,128]{3,1,2,0:T(4,128)S(1)}, f32[4,4,32,128]{3,1,2,0:T(4,128)}, u32[]{:S(2)}, u32[]{:S(2)}) collective-permute-start(f32[4,4,32,128]{3,1,2,0:T(4,128)S(1)} %get-tuple-element.27), channel_id=1, source_target_pairs={{16,0},{32,16},{48,32},{64,48},{80,64},{96,80},{112,96},{128,112},... | collective-permute-start | bytes 786440 | tf_op jit(solution)/shard_map/ppermute | solution.py:29
  32.5 2.8 %reduce = f32[16,8192]{1,0:T(8,128)} reduce(f32[16,1,8192]{2,1,0:T(1,128)S(1)} %all-to-all-done, f32[]{:T(128)} %broadcast.6), dimensions={1}, to_apply=%all_to_all.52.reduce_sub_computation | reduce | bytes 1048580 | tf_op jit(solution)/shard_map/all_to_all | solution.py:145
  37.0 2.6 %copy.105 = f32[4,8,16,32,8]{3,2,4,1,0:T(8,128)} copy(f32[4,8,16,32,8]{3,1,0,4,2:T(8,128)S(1)} %bitcast.281) | data formatting | bytes 1048576 | tf_op jit(solution)/shard_map/all_to_all | solution.py:145
  43.0 7.4 %copy.106 = f32[4,8,8,512]{2,1,0,3:T(8,128)} copy(f32[4,8,8,512]{3,2,1,0:T(8,128)S(1)} %fusion.27) | data formatting | bytes 1048576 | tf_op jit(solution)/shard_map/fack,jk->facj/dot_general | solution.py:147
  50.5 7.3 %reshape.18 = f32[16,1,8192]{2,1,0:T(1,128)} reshape(f32[512,4,8,8]{3,2,1,0:T(8,128)} %bitcast.271) | data formatting | bytes 1048576
  57.8 8.2 %all-to-all-start.1 = ((f32[16,1,8192]{2,1,0:T(1,128)}), f32[16,1,8192]{2,1,0:T(1,128)S(1)}, u32[]{:S(2)}, u32[]{:S(2)}) async-start(f32[16,1,8192]{2,1,0:T(1,128)} %reshape.18), calls=%async_computation.1 | async-start | bytes 1048576 | tf_op jit(solution)/shard_map/all_to_all | solution.py:148
  68.1 2.7 %convolution_bitcast_fusion = f32[4,8,32,128]{3,1,2,0:T(8,128)} fusion(f32[8,16,1,1]{1,0,3,2:T(8,128)S(1)} %copy-done.23, f32[4,4,32,128]{3,1,2,0:T(4,128)} %collective-permute-done.1, f32[1,8,32,128]{3,1,2,0:T(8,128)S(1)} %bitcast.275, f32[3,8,32,128]{3,1,2,0:T(8,128)S(1)} %get-tuple-element.28, f32[4,4,32,128]{3,1,2,0:T(4,128)} %collective-permute-done), kind=kOutput, calls=%fused_computation.10 | convolution fusion | flops 25952256 | bytes 1573376 | tf_op jit(solution)/shard_map/il,flab->fiab/dot_general | solution.py:133
  70.8 4.5 %all-to-all-done.1 = f32[16,1,8192]{2,1,0:T(1,128)S(1)} async-done(((f32[16,1,8192]{2,1,0:T(1,128)}), f32[16,1,8192]{2,1,0:T(1,128)S(1)}, u32[]{:S(2)}, u32[]{:S(2)}) %all-to-all-start.1) | async-done | bytes 524320 | tf_op jit(solution)/shard_map/all_to_all | solution.py:148
  77.2 6.7 %reshape.19 = f32[512,4,8,8]{3,2,1,0:T(8,128)} reshape(f32[16,8192]{1,0:T(8,128)S(1)} %reduce.1) | data formatting | bytes 1048576
  83.9 5.2 %copy.107 = f32[4,8,8,16,32]{4,2,3,1,0:T(8,128)S(1)} copy(f32[4,8,8,16,32]{2,1,0,4,3:T(8,128)} %bitcast.270) | data formatting | bytes 1048576 | tf_op jit(solution)/shard_map/all_to_all | solution.py:148
  103.7 6.8 %all-to-all-start.2 = ((f32[16,1,10240]{2,1,0:T(1,128)}), f32[16,1,10240]{2,1,0:T(1,128)S(1)}, u32[]{:S(2)}, u32[]{:S(2)}) async-start(f32[16,1,10240]{2,1,0:T(1,128)} %reshape.20), calls=%async_computation.2 | async-start | bytes 1310720 | tf_op jit(solution)/shard_map/all_to_all | solution.py:145
  113.2 7.9 %all-to-all-done.2 = f32[16,1,10240]{2,1,0:T(1,128)S(1)} async-done(((f32[16,1,10240]{2,1,0:T(1,128)}), f32[16,1,10240]{2,1,0:T(1,128)S(1)}, u32[]{:S(2)}, u32[]{:S(2)}) %all-to-all-start.2) | async-done | bytes 655392 | tf_op jit(solution)/shard_map/all_to_all | solution.py:145
  121.2 3.2 %reduce.2 = f32[16,10240]{1,0:T(8,128)} reduce(f32[16,1,10240]{2,1,0:T(1,128)S(1)} %all-to-all-done.2, f32[]{:T(128)} %broadcast.6), dimensions={1}, to_apply=%all_to_all.60.reduce_sub_computation | reduce | bytes 1310724 | tf_op jit(solution)/shard_map/all_to_all | solution.py:145
  126.3 3.0 %copy.119 = f32[5,8,16,32,8]{3,2,4,1,0:T(8,128)} copy(f32[5,8,16,32,8]{3,1,0,4,2:T(8,128)S(1)} %bitcast.277) | data formatting | bytes 1310720 | tf_op jit(solution)/shard_map/all_to_all | solution.py:145
  133.1 5.5 %copy.120 = f32[5,8,8,512]{2,1,0,3:T(8,128)} copy(f32[5,8,8,512]{3,2,1,0:T(8,128)S(1)} %fusion.25) | data formatting | bytes 1310720 | tf_op jit(solution)/shard_map/fack,jk->facj/dot_general | solution.py:147
  138.6 9.1 %reshape.22 = f32[16,1,10240]{2,1,0:T(1,128)} reshape(f32[512,5,8,8]{3,2,1,0:T(8,128)} %bitcast.268) | data formatting | bytes 1310720
  147.8 6.8 %all-to-all-start.3 = ((f32[16,1,10240]{2,1,0:T(1,128)}), f32[16,1,10240]{2,1,0:T(1,128)S(1)}, u32[]{:S(2)}, u32[]{:S(2)}) async-start(f32[16,1,10240]{2,1,0:T(1,128)} %reshape.22), calls=%async_computation.3 | async-start | bytes 1310720 | tf_op jit(solution)/shard_map/all_to_all | solution.py:148
  156.5 5.7 %collective-permute-start.3 = (f32[5,4,32,128]{3,1,2,0:T(4,128)}, f32[5,4,32,128]{3,1,2,0:T(4,128)}, u32[]{:S(2)}, u32[]{:S(2)}) collective-permute-start(f32[5,4,32,128]{3,1,2,0:T(4,128)} %get-tuple-element.25), channel_id=1, source_target_pairs={{16,0},{32,16},{48,32},{64,48},{80,64},{96,80},{112,96},{128,112},... | collective-permute-start | bytes 983048 | tf_op jit(solution)/shard_map/ppermute | solution.py:29
  164.0 8.5 %all-to-all-done.3 = f32[16,1,10240]{2,1,0:T(1,128)S(1)} async-done(((f32[16,1,10240]{2,1,0:T(1,128)}), f32[16,1,10240]{2,1,0:T(1,128)S(1)}, u32[]{:S(2)}, u32[]{:S(2)}) %all-to-all-start.3) | async-done | bytes 655392 | tf_op jit(solution)/shard_map/all_to_all | solution.py:148
  174.7 10.4 %reshape.23 = f32[512,5,8,8]{3,2,1,0:T(8,128)} reshape(f32[16,10240]{1,0:T(8,128)S(1)} %reduce.3) | data formatting | bytes 1310720
  185.2 6.6 %copy.121 = f32[5,8,8,16,32]{4,2,3,1,0:T(8,128)S(1)} copy(f32[5,8,8,16,32]{2,1,0,4,3:T(8,128)} %bitcast.269) | data formatting | bytes 1310720 | tf_op jit(solution)/shard_map/all_to_all | solution.py:148
  193.7 2.8 %maximum_add_fusion = (f32[5,8,32,128]{3,1,2,0:T(8,128)S(1)}, f32[5,8,32,128]{3,1,2,0:T(8,128)S(1)}) fusion(f32[1,8,32,128]{3,1,2,0:T(8,128)S(1)} %copy-done.20, f32[3,8,32,128]{3,1,2,0:T(8,128)S(1)} %get-tuple-element.32, f32[1,8,32,128]{3,1,2,0:T(8,128)S(1)} %copy-done.19, f32[5,8,128,32]{2,1,3,0:T(8,128)} %copy.122, f32[5,8,32,128]{3,1,2,0:T(8,128)} %fusion.71, ...), kind=kOutput, calls=%fused_computation.21 | convolution fusion | flops 33259520 | bytes 4588032 | tf_op jit(solution)/shard_map/il,flab->fiab/dot_general | solution.py:133
  (90 shorter events, 51.7 us)
Async XLA Ops:
  4.7 93.1 %copy-start = (f32[8,32,128]{2,0,1:T(8,128)}, f32[8,32,128]{2,0,1:T(8,128)S(1)}, u32[]{:S(2)}) copy-start(f32[8,32,128]{2,0,1:T(8,128)S(1)} %get-tuple-element.19) | copy-start | bytes 393220
  10.2 21.7 %all-to-all-start = ((f32[16,1,8192]{2,1,0:T(1,128)}), f32[16,1,8192]{2,1,0:T(1,128)S(1)}, u32[]{:S(2)}, u32[]{:S(2)}) async-start(f32[16,1,8192]{2,1,0:T(1,128)} %reshape.16), calls=%async_computation | async-start | bytes 1048576 | tf_op jit(solution)/shard_map/all_to_all | solution.py:145
  20.6 47.5 %collective-permute-start = (f32[4,4,32,128]{3,1,2,0:T(4,128)}, f32[4,4,32,128]{3,1,2,0:T(4,128)}, u32[]{:S(2)}, u32[]{:S(2)}) collective-permute-start(f32[4,4,32,128]{3,1,2,0:T(4,128)} %get-tuple-element.26), channel_id=1, source_target_pairs={{0,16},{16,32},{32,48},{48,64},{64,80},{80,96},{96,112},{112,128},... | collective-permute-start | bytes 786440 | tf_op jit(solution)/shard_map/ppermute | solution.py:28
  22.5 45.6 %collective-permute-start.1 = (f32[4,4,32,128]{3,1,2,0:T(4,128)S(1)}, f32[4,4,32,128]{3,1,2,0:T(4,128)}, u32[]{:S(2)}, u32[]{:S(2)}) collective-permute-start(f32[4,4,32,128]{3,1,2,0:T(4,128)S(1)} %get-tuple-element.27), channel_id=1, source_target_pairs={{16,0},{32,16},{48,32},{64,48},{80,64},{96,80},{112,96},{128,112},... | collective-permute-start | bytes 786440 | tf_op jit(solution)/shard_map/ppermute | solution.py:29
  50.5 16.2 %copy-start.21 = (f32[128,128,1,1]{1,0,3,2:T(8,128)S(1)}, f32[128,128,1,1]{1,0,3,2:T(8,128)}, u32[]{:S(2)}) copy-start(f32[128,128,1,1]{1,0,3,2:T(8,128)} %constant.34) | copy-start | bytes 196612
  57.8 10.3 %copy-start.23 = (f32[8,16,1,1]{1,0,3,2:T(8,128)S(1)}, f32[8,16,1,1]{1,0,3,2:T(8,128)}, u32[]{:S(2)}) copy-start(f32[8,16,1,1]{1,0,3,2:T(8,128)} %constant.33) | copy-start | bytes 1540
  57.8 17.5 %all-to-all-start.1 = ((f32[16,1,8192]{2,1,0:T(1,128)}), f32[16,1,8192]{2,1,0:T(1,128)S(1)}, u32[]{:S(2)}, u32[]{:S(2)}) async-start(f32[16,1,8192]{2,1,0:T(1,128)} %reshape.18), calls=%async_computation.1 | async-start | bytes 1048576 | tf_op jit(solution)/shard_map/all_to_all | solution.py:148
  90.4 5.4 %copy-start.16 = (f32[4,8,32,128]{3,1,2,0:T(8,128)S(1)}, f32[4,8,32,128]{3,1,2,0:T(8,128)}, u32[]{:S(2)}) copy-start(f32[4,8,32,128]{3,1,2,0:T(8,128)} %convolution_bitcast_fusion) | copy-start | bytes 1572868
  93.9 3.9 %copy-start.10 = (f32[8,32,128]{2,0,1:T(8,128)}, f32[8,32,128]{2,0,1:T(8,128)S(1)}, u32[]{:S(2)}) copy-start(f32[8,32,128]{2,0,1:T(8,128)S(1)} %get-tuple-element.13) | copy-start | bytes 393220
  93.9 3.9 %copy-start.9 = (f32[4,8,128,32]{2,1,3,0:T(8,128)S(1)}, f32[4,8,128,32]{2,1,3,0:T(8,128)}, u32[]{:S(2)}) copy-start(f32[4,8,128,32]{2,1,3,0:T(8,128)} %copy.108) | copy-start | bytes 1572868
  93.9 3.9 %copy-start.14 = (f32[8,32,128]{2,1,0:T(8,128)S(1)}, f32[8,32,128]{2,1,0:T(8,128)}, u32[]{:S(2)}) copy-start(f32[8,32,128]{2,1,0:T(8,128)} %param.8) | copy-start | bytes 393220
  103.7 8.6 %copy-start.8 = (f32[5,8,32,128]{3,1,2,0:T(8,128)S(1)}, f32[5,8,32,128]{3,1,2,0:T(8,128)}, u32[]{:S(2)}) copy-start(f32[5,8,32,128]{3,1,2,0:T(8,128)} %copy-done.7) | copy-start | bytes 1966084
  103.7 17.4 %all-to-all-start.2 = ((f32[16,1,10240]{2,1,0:T(1,128)}), f32[16,1,10240]{2,1,0:T(1,128)S(1)}, u32[]{:S(2)}, u32[]{:S(2)}) async-start(f32[16,1,10240]{2,1,0:T(1,128)} %reshape.20), calls=%async_computation.2 | async-start | bytes 1310720 | tf_op jit(solution)/shard_map/all_to_all | solution.py:145
  138.6 16.0 %copy-start.11 = (f32[8,32,128]{2,0,1:T(8,128)S(1)}, f32[8,32,128]{2,0,1:T(8,128)}, u32[]{:S(2)}) copy-start(f32[8,32,128]{2,0,1:T(8,128)} %copy-done.10) | copy-start | bytes 393220
  138.6 16.0 %copy-start.18 = (f32[5,8,32,128]{3,1,2,0:T(8,128)S(1)}, f32[5,8,32,128]{3,1,2,0:T(8,128)}, u32[]{:S(2)}) copy-start(f32[5,8,32,128]{3,1,2,0:T(8,128)} %bitcast_dynamic-update-slice_fusion.4) | copy-start | bytes 1966084
  138.6 23.7 %copy-start.1 = (f32[8,32,128]{2,0,1:T(8,128)S(1)}, f32[8,32,128]{2,0,1:T(8,128)}, u32[]{:S(2)}) copy-start(f32[8,32,128]{2,0,1:T(8,128)} %copy-done) | copy-start | bytes 393220
  138.6 23.7 %copy-start.5 = (f32[8,32,128]{2,0,1:T(8,128)S(1)}, f32[8,32,128]{2,0,1:T(8,128)}, u32[]{:S(2)}) copy-start(f32[8,32,128]{2,0,1:T(8,128)} %copy-done.4) | copy-start | bytes 393220
  138.6 23.7 %copy-start.6 = (f32[4,8,32,128]{3,1,2,0:T(8,128)S(1)}, f32[4,8,32,128]{3,1,2,0:T(8,128)}, u32[]{:S(2)}) copy-start(f32[4,8,32,128]{3,1,2,0:T(8,128)} %fusion.66) | copy-start | bytes 1572868
  138.6 23.7 %copy-start.13 = (f32[8,32,128]{2,0,1:T(8,128)S(1)}, f32[8,32,128]{2,0,1:T(8,128)}, u32[]{:S(2)}) copy-start(f32[8,32,128]{2,0,1:T(8,128)} %copy-done.12) | copy-start | bytes 393220
  138.6 23.7 %copy-start.15 = (f32[8,32,128]{2,1,0:T(8,128)S(1)}, f32[8,32,128]{2,1,0:T(8,128)}, u32[]{:S(2)}) copy-start(f32[8,32,128]{2,1,0:T(8,128)} %param.8) | copy-start | bytes 393220
  147.8 14.7 %copy-start.22 = (f32[128,128,1,1]{1,0,3,2:T(8,128)S(1)}, f32[128,128,1,1]{1,0,3,2:T(8,128)}, u32[]{:S(2)}) copy-start(f32[128,128,1,1]{1,0,3,2:T(8,128)} %constant.34) | copy-start | bytes 196612
  147.8 24.8 %all-to-all-start.3 = ((f32[16,1,10240]{2,1,0:T(1,128)}), f32[16,1,10240]{2,1,0:T(1,128)S(1)}, u32[]{:S(2)}, u32[]{:S(2)}) async-start(f32[16,1,10240]{2,1,0:T(1,128)} %reshape.22), calls=%async_computation.3 | async-start | bytes 1310720 | tf_op jit(solution)/shard_map/all_to_all | solution.py:148
  154.6 39.0 %collective-permute-start.2 = (f32[5,4,32,128]{3,1,2,0:T(4,128)}, f32[5,4,32,128]{3,1,2,0:T(4,128)}, u32[]{:S(2)}, u32[]{:S(2)}) collective-permute-start(f32[5,4,32,128]{3,1,2,0:T(4,128)} %get-tuple-element.24), channel_id=1, source_target_pairs={{0,16},{16,32},{32,48},{48,64},{64,80},{80,96},{96,112},{112,128},... | collective-permute-start | bytes 983048 | tf_op jit(solution)/shard_map/ppermute | solution.py:28
  156.5 37.1 %collective-permute-start.3 = (f32[5,4,32,128]{3,1,2,0:T(4,128)}, f32[5,4,32,128]{3,1,2,0:T(4,128)}, u32[]{:S(2)}, u32[]{:S(2)}) collective-permute-start(f32[5,4,32,128]{3,1,2,0:T(4,128)} %get-tuple-element.25), channel_id=1, source_target_pairs={{16,0},{32,16},{48,32},{64,48},{80,64},{96,80},{112,96},{128,112},... | collective-permute-start | bytes 983048 | tf_op jit(solution)/shard_map/ppermute | solution.py:29
  (8 other events, 15.1 us)
where the time goes:
time: 200 us; the launch traced here: 198 us
  local copies, waits for them, and re-layouts  91.3 us (46%)
  starting transfers between devices  50.4 us (25%)
  other arithmetic  24.1 us (12%)
  waiting for transfers between devices  20.9 us (10%)
  matrix products  10.7 us (5%)
    unnamed x60, local copies, waits for them, and re-layouts  46.2 us
    all_to_all x2, starting transfers between devices, derive_span(): lax.all_to_all(values, 'gy', split_axis=3, concat_axis=2, tiled=True)  16.4 us
    ppermute x2, starting transfers between devices, padded(): after = lax.ppermute(initial, axis, down)  15.1 us
    all_to_all x2, starting transfers between devices, derive_span(): lax.all_to_all(derived, 'gy', split_axis=3, concat_axis=2, tiled=True)  15 us
    all_to_all x4, local copies, waits for them, and re-layouts, derive_span(): lax.all_to_all(derived, 'gy', split_axis=3, concat_axis=2, tiled=True)  15 us
    all_to_all x2, waiting for transfers between devices, derive_span(): lax.all_to_all(derived, 'gy', split_axis=3, concat_axis=2, tiled=True)  13 us
    dot_general x2, local copies, waits for them, and re-layouts, derive_span(): derived = jnp.einsum('fack,jk->facj', lines, z_matrix, precision=highest)  12.9 us
    all_to_all x5, local copies, waits for them, and re-layouts, derive_span(): lax.all_to_all(values, 'gy', split_axis=3, concat_axis=2, tiled=True)  11.1 us
  transfers between devices with their start and end apart: 8, of which 3 were waited for; matrix products, arithmetic and copies ran while one was open for 27% of the time, Pallas kernels for 0%

commit v1 on v0

--- a/solution.py
+++ b/solution.py
@@ -145,7 +145,19 @@
             lax.all_to_all(values, "gy", split_axis=3, concat_axis=2, tiled=True), (0, 1, 3, 2)
         )
         derived = jnp.einsum("fack,jk->facj", lines, z_matrix, precision=highest)
-        returned = lax.all_to_all(derived, "gy", split_axis=3, concat_axis=2, tiled=True)
+
+        def deliver_limits_all(array_in, peer_axis):
+            return jnp.concatenate(
+                lax.all_to_all(
+                    jnp.stack(jnp.split(array_in, lax.axis_size(peer_axis), 3)),
+                    axis_name=peer_axis,
+                    split_axis=0,
+                    concat_axis=0,
+                ),
+                2,
+            )
+
+        returned = deliver_limits_all(derived, "gy")
         return jnp.transpose(returned, (0, 1, 3, 2))
 
     def gradients_of(basic_quantities):

time: 200 us -> 168 us (0.84)
  local copies, waits for them, and re-layouts: 91.3 us -> 60.3 us
    all_to_all x4 -> x0, local copies, waits for them, and re-layouts: 15 us -> none  [derive_span(): lax.all_to_all(derived, 'gy', split_axis=3, concat_axis=2, tiled=True)]
    dot_general x2 -> x0, local copies, waits for them, and re-layouts: 12.9 us -> none  [derive_span(): derived = jnp.einsum('fack,jk->facj', lines, z_matrix, precision=highest)]
    unnamed x60 -> x94, local copies, waits for them, and re-layouts: 46.2 us -> 33.9 us
    reshape x0 -> x4, local copies, waits for them, and re-layouts: none -> 8.38 us  [deliver_limits_all(): jnp.concatenate(lax.all_to_all(jnp.stack(jnp.split(array_in, lax.axis_siz...]
    unnamed x8, other arithmetic: 8.32 us -> 6.26 us
  transfers between devices with their start and end apart: 8 -> 8, of which waited for: 3 -> 3; matrix products, arithmetic and copies ran while one was open for 27% -> 19% of each run, Pallas kernels for 0% -> 0%
where the time goes in v1:
time: 168 us; the launch traced here: 167 us
  local copies, waits for them, and re-layouts  60.3 us (36%)
  starting transfers between devices  50.2 us (30%)
  other arithmetic  24 us (14%)
  waiting for transfers between devices  21 us (12%)
  matrix products  10 us (6%)
    unnamed x94, local copies, waits for them, and re-layouts  33.9 us
    all_to_all x2, starting transfers between devices, derive_span(): lax.all_to_all(values, 'gy', split_axis=3, concat_axis=2, tiled=True)  16.4 us
    ppermute x2, starting transfers between devices, padded(): after = lax.ppermute(initial, axis, down)  15.1 us
    all_to_all x2, starting transfers between devices, deliver_limits_all(): lax.all_to_all(jnp.stack(jnp.split(array_in, lax.axis_size(peer_axis), 3)...  14.9 us
    all_to_all x2, waiting for transfers between devices, deliver_limits_all(): lax.all_to_all(jnp.stack(jnp.split(array_in, lax.axis_size(peer_axis), 3)...  13.1 us
    all_to_all x5, local copies, waits for them, and re-layouts, derive_span(): lax.all_to_all(values, 'gy', split_axis=3, concat_axis=2, tiled=True)  11.1 us
    reshape x4, local copies, waits for them, and re-layouts, deliver_limits_all(): jnp.concatenate(lax.all_to_all(jnp.stack(jnp.split(array_in, lax.axis_siz...  8.38 us
    all_to_all x2, waiting for transfers between devices, derive_span(): lax.all_to_all(values, 'gy', split_axis=3, concat_axis=2, tiled=True)  7.93 us
  transfers between devices with their start and end apart: 8, of which 3 were waited for; matrix products, arithmetic and copies ran while one was open for 19% of the time, Pallas kernels for 0%

profile of v1, /device:TPU:7, one launch (start us, length us, event | category | flops | bytes accessed | tf_op | source)
XLA Modules:
  0.0 166.6 jit_solution(9277754265185258246)
XLA Ops:
  5.6 2.9 %copy.101 = f32[4,8,32,128]{2,1,0,3:T(8,128)S(1)} copy(f32[4,8,32,128]{3,1,2,0:T(8,128)} %pad_maximum_fusion) | data formatting | bytes 1048576 | tf_op jit(solution)/shard_map/concatenate | solution.py:88
  10.2 9.6 %all-to-all-start = ((f32[16,1,8192]{2,1,0:T(1,128)}), f32[16,1,8192]{2,1,0:T(1,128)S(1)}, u32[]{:S(2)}, u32[]{:S(2)}) async-start(f32[16,1,8192]{2,1,0:T(1,128)} %reshape.32), calls=%async_computation | async-start | bytes 1048576 | tf_op jit(solution)/shard_map/all_to_all | solution.py:145
  22.5 9.4 %collective-permute-start.1 = (f32[4,4,32,128]{3,1,2,0:T(4,128)S(1)}, f32[4,4,32,128]{3,1,2,0:T(4,128)}, u32[]{:S(2)}, u32[]{:S(2)}) collective-permute-start(f32[4,4,32,128]{3,1,2,0:T(4,128)S(1)} %get-tuple-element.27), channel_id=1, source_target_pairs={{16,0},{32,16},{48,32},{64,48},{80,64},{96,80},{112,96},{128,112},... | collective-permute-start | bytes 786440 | tf_op jit(solution)/shard_map/ppermute | solution.py:29
  32.5 2.8 %reduce = f32[16,8192]{1,0:T(8,128)} reduce(f32[16,1,8192]{2,1,0:T(1,128)S(1)} %all-to-all-done, f32[]{:T(128)} %broadcast.6), dimensions={1}, to_apply=%all_to_all.32.reduce_sub_computation | reduce | bytes 1048580 | tf_op jit(solution)/shard_map/all_to_all | solution.py:145
  37.0 2.6 %copy.103 = f32[4,8,16,32,8]{3,2,4,1,0:T(8,128)} copy(f32[4,8,16,32,8]{3,1,0,4,2:T(8,128)S(1)} %bitcast.401) | data formatting | bytes 1048576 | tf_op jit(solution)/shard_map/all_to_all | solution.py:145
  39.5 2.4 %all_to_all.35 = f32[4,8,512,8]{2,3,1,0:T(8,128)S(1)} reshape(f32[4,8,16,32,8]{3,2,4,1,0:T(8,128)} %copy.103) | data formatting | bytes 1048576 | tf_op jit(solution)/shard_map/all_to_all | solution.py:145
  46.1 8.1 %all-to-all-start.1 = ((f32[16,1,8192]{2,1,0:T(1,128)}), f32[16,1,8192]{2,1,0:T(1,128)S(1)}, u32[]{:S(2)}, u32[]{:S(2)}) async-start(f32[16,1,8192]{2,1,0:T(1,128)} %reshape.34), calls=%async_computation.1 | async-start | bytes 1048576 | tf_op jit(solution)/shard_map/all_to_all | solution.py:151
  56.2 2.7 %convolution_bitcast_fusion = f32[4,8,32,128]{3,1,2,0:T(8,128)} fusion(f32[8,16,1,1]{1,0,3,2:T(8,128)S(1)} %copy-done.25, f32[4,4,32,128]{3,1,2,0:T(4,128)} %collective-permute-done.1, f32[1,8,32,128]{3,1,2,0:T(8,128)S(1)} %bitcast.397, f32[3,8,32,128]{3,1,2,0:T(8,128)S(1)} %get-tuple-element.28, f32[4,4,32,128]{3,1,2,0:T(4,128)} %collective-permute-done), kind=kOutput, calls=%fused_computation.12 | convolution fusion | flops 25952256 | bytes 1573376 | tf_op jit(solution)/shard_map/il,flab->fiab/dot_general | solution.py:133
  58.9 4.6 %all-to-all-done.1 = f32[16,1,8192]{2,1,0:T(1,128)S(1)} async-done(((f32[16,1,8192]{2,1,0:T(1,128)}), f32[16,1,8192]{2,1,0:T(1,128)S(1)}, u32[]{:S(2)}, u32[]{:S(2)}) %all-to-all-start.1) | async-done | bytes 524320 | tf_op jit(solution)/shard_map/all_to_all | solution.py:151
  63.5 2.8 %reduce.1 = f32[16,8192]{1,0:T(8,128)} reduce(f32[16,1,8192]{2,1,0:T(1,128)S(1)} %all-to-all-done.1, f32[]{:T(128)} %broadcast.6), dimensions={1}, to_apply=%all_to_all.36.reduce_sub_computation | reduce | bytes 1048580 | tf_op jit(solution)/shard_map/all_to_all | solution.py:151
  69.6 2.2 %copy.105 = f32[4,8,128,32]{2,1,3,0:T(8,128)S(1)} copy(f32[4,8,128,32]{3,2,1,0:T(8,128)} %copy_bitcast_fusion.1) | data formatting | bytes 1048576 | tf_op jit(solution)/shard_map/reshape | solution.py:150
  78.9 2.2 %copy.114 = f32[5,8,32,128]{2,1,0,3:T(8,128)S(1)} copy(f32[5,8,32,128]{3,1,2,0:T(8,128)} %get-tuple-element.20) | data formatting | bytes 1310720 | tf_op jit(solution)/shard_map/stack | solution.py:121
  83.0 6.8 %all-to-all-start.2 = ((f32[16,1,10240]{2,1,0:T(1,128)}), f32[16,1,10240]{2,1,0:T(1,128)S(1)}, u32[]{:S(2)}, u32[]{:S(2)}) async-start(f32[16,1,10240]{2,1,0:T(1,128)} %reshape.36), calls=%async_computation.2 | async-start | bytes 1310720 | tf_op jit(solution)/shard_map/all_to_all | solution.py:145
  92.6 7.9 %all-to-all-done.2 = f32[16,1,10240]{2,1,0:T(1,128)S(1)} async-done(((f32[16,1,10240]{2,1,0:T(1,128)}), f32[16,1,10240]{2,1,0:T(1,128)S(1)}, u32[]{:S(2)}, u32[]{:S(2)}) %all-to-all-start.2) | async-done | bytes 655392 | tf_op jit(solution)/shard_map/all_to_all | solution.py:145
  100.5 3.2 %reduce.2 = f32[16,10240]{1,0:T(8,128)} reduce(f32[16,1,10240]{2,1,0:T(1,128)S(1)} %all-to-all-done.2, f32[]{:T(128)} %broadcast.6), dimensions={1}, to_apply=%all_to_all.37.reduce_sub_computation | reduce | bytes 1310724 | tf_op jit(solution)/shard_map/all_to_all | solution.py:145
  105.6 3.0 %copy.116 = f32[5,8,16,32,8]{3,2,4,1,0:T(8,128)} copy(f32[5,8,16,32,8]{3,1,0,4,2:T(8,128)S(1)} %bitcast.399) | data formatting | bytes 1310720 | tf_op jit(solution)/shard_map/all_to_all | solution.py:145
  108.6 2.6 %all_to_all.40 = f32[5,8,512,8]{2,3,1,0:T(8,128)S(1)} reshape(f32[5,8,16,32,8]{3,2,4,1,0:T(8,128)} %copy.116) | data formatting | bytes 1310720 | tf_op jit(solution)/shard_map/all_to_all | solution.py:145
  124.6 3.5 %reshape.38 = f32[16,1,10240]{2,1,0:T(1,128)} reshape(f32[16,5,8,8,32]{4,3,2,1,0:T(8,128)} %fusion.31) | data formatting | bytes 1310720
  128.1 6.8 %all-to-all-start.3 = ((f32[16,1,10240]{2,1,0:T(1,128)}), f32[16,1,10240]{2,1,0:T(1,128)S(1)}, u32[]{:S(2)}, u32[]{:S(2)}) async-start(f32[16,1,10240]{2,1,0:T(1,128)} %reshape.38), calls=%async_computation.3 | async-start | bytes 1310720 | tf_op jit(solution)/shard_map/all_to_all | solution.py:151
  136.8 5.7 %collective-permute-start.3 = (f32[5,4,32,128]{3,1,2,0:T(4,128)}, f32[5,4,32,128]{3,1,2,0:T(4,128)}, u32[]{:S(2)}, u32[]{:S(2)}) collective-permute-start(f32[5,4,32,128]{3,1,2,0:T(4,128)} %get-tuple-element.25), channel_id=1, source_target_pairs={{16,0},{32,16},{48,32},{64,48},{80,64},{96,80},{112,96},{128,112},... | collective-permute-start | bytes 983048 | tf_op jit(solution)/shard_map/ppermute | solution.py:29
  144.3 8.5 %all-to-all-done.3 = f32[16,1,10240]{2,1,0:T(1,128)S(1)} async-done(((f32[16,1,10240]{2,1,0:T(1,128)}), f32[16,1,10240]{2,1,0:T(1,128)S(1)}, u32[]{:S(2)}, u32[]{:S(2)}) %all-to-all-start.3) | async-done | bytes 655392 | tf_op jit(solution)/shard_map/all_to_all | solution.py:151
  152.9 3.2 %reduce.3 = f32[16,10240]{1,0:T(8,128)} reduce(f32[16,1,10240]{2,1,0:T(1,128)S(1)} %all-to-all-done.3, f32[]{:T(128)} %broadcast.6), dimensions={1}, to_apply=%all_to_all.41.reduce_sub_computation | reduce | bytes 1310724 | tf_op jit(solution)/shard_map/all_to_all | solution.py:151
  159.8 2.7 %copy.118 = f32[5,8,128,32]{2,1,3,0:T(8,128)S(1)} copy(f32[5,8,128,32]{3,2,1,0:T(8,128)} %copy_bitcast_fusion) | data formatting | bytes 1310720 | tf_op jit(solution)/shard_map/reshape | solution.py:150
  162.6 2.2 %maximum_add_fusion = (f32[5,8,32,128]{3,1,2,0:T(8,128)S(1)}, f32[5,8,32,128]{3,1,2,0:T(8,128)S(1)}) fusion(f32[1,8,32,128]{3,1,2,0:T(8,128)S(1)} %copy-done.22, f32[3,8,32,128]{3,1,2,0:T(8,128)S(1)} %get-tuple-element.32, f32[1,8,32,128]{3,1,2,0:T(8,128)S(1)} %copy-done.21, f32[5,8,128,32]{2,1,3,0:T(8,128)S(1)} %copy.118, ...), kind=kOutput, calls=%fused_computation.23 | convolution fusion | flops 33259520 | bytes 4588032 | tf_op jit(solution)/shard_map/il,flab->fiab/dot_general | solution.py:133
  (124 shorter events, 57.4 us)
Async XLA Ops:
  4.8 72.4 %copy-start = (f32[8,32,128]{2,0,1:T(8,128)}, f32[8,32,128]{2,0,1:T(8,128)S(1)}, u32[]{:S(2)}) copy-start(f32[8,32,128]{2,0,1:T(8,128)S(1)} %get-tuple-element.19) | copy-start | bytes 393220
  10.2 21.7 %all-to-all-start = ((f32[16,1,8192]{2,1,0:T(1,128)}), f32[16,1,8192]{2,1,0:T(1,128)S(1)}, u32[]{:S(2)}, u32[]{:S(2)}) async-start(f32[16,1,8192]{2,1,0:T(1,128)} %reshape.32), calls=%async_computation | async-start | bytes 1048576 | tf_op jit(solution)/shard_map/all_to_all | solution.py:145
  20.6 35.6 %collective-permute-start = (f32[4,4,32,128]{3,1,2,0:T(4,128)}, f32[4,4,32,128]{3,1,2,0:T(4,128)}, u32[]{:S(2)}, u32[]{:S(2)}) collective-permute-start(f32[4,4,32,128]{3,1,2,0:T(4,128)} %get-tuple-element.26), channel_id=1, source_target_pairs={{0,16},{16,32},{32,48},{48,64},{64,80},{80,96},{96,112},{112,128},... | collective-permute-start | bytes 786440 | tf_op jit(solution)/shard_map/ppermute | solution.py:28
  22.5 33.7 %collective-permute-start.1 = (f32[4,4,32,128]{3,1,2,0:T(4,128)S(1)}, f32[4,4,32,128]{3,1,2,0:T(4,128)}, u32[]{:S(2)}, u32[]{:S(2)}) collective-permute-start(f32[4,4,32,128]{3,1,2,0:T(4,128)S(1)} %get-tuple-element.27), channel_id=1, source_target_pairs={{16,0},{32,16},{48,32},{64,48},{80,64},{96,80},{112,96},{128,112},... | collective-permute-start | bytes 786440 | tf_op jit(solution)/shard_map/ppermute | solution.py:29
  44.2 10.6 %copy-start.23 = (f32[128,128,1,1]{1,0,3,2:T(8,128)S(1)}, f32[128,128,1,1]{1,0,3,2:T(8,128)}, u32[]{:S(2)}) copy-start(f32[128,128,1,1]{1,0,3,2:T(8,128)} %constant.34) | copy-start | bytes 196612
  44.3 11.9 %copy-start.25 = (f32[8,16,1,1]{1,0,3,2:T(8,128)S(1)}, f32[8,16,1,1]{1,0,3,2:T(8,128)}, u32[]{:S(2)}) copy-start(f32[8,16,1,1]{1,0,3,2:T(8,128)} %constant.33) | copy-start | bytes 1540
  46.1 17.4 %all-to-all-start.1 = ((f32[16,1,8192]{2,1,0:T(1,128)}), f32[16,1,8192]{2,1,0:T(1,128)S(1)}, u32[]{:S(2)}, u32[]{:S(2)}) async-start(f32[16,1,8192]{2,1,0:T(1,128)} %reshape.34), calls=%async_computation.1 | async-start | bytes 1048576 | tf_op jit(solution)/shard_map/all_to_all | solution.py:151
  69.6 4.0 %copy-start.6 = (f32[4,8,32,128]{3,1,2,0:T(8,128)S(1)}, f32[4,8,32,128]{3,1,2,0:T(8,128)}, u32[]{:S(2)}) copy-start(f32[4,8,32,128]{3,1,2,0:T(8,128)} %fusion.98) | copy-start | bytes 1572868
  71.8 4.2 %copy-start.18 = (f32[4,8,32,128]{3,1,2,0:T(8,128)S(1)}, f32[4,8,32,128]{3,1,2,0:T(8,128)}, u32[]{:S(2)}) copy-start(f32[4,8,32,128]{3,1,2,0:T(8,128)} %convolution_bitcast_fusion) | copy-start | bytes 1572868
  74.3 2.9 %copy-start.12 = (f32[8,32,128]{2,0,1:T(8,128)}, f32[8,32,128]{2,0,1:T(8,128)S(1)}, u32[]{:S(2)}) copy-start(f32[8,32,128]{2,0,1:T(8,128)S(1)} %get-tuple-element.13) | copy-start | bytes 393220
  74.3 2.9 %copy-start.16 = (f32[8,32,128]{2,1,0:T(8,128)S(1)}, f32[8,32,128]{2,1,0:T(8,128)}, u32[]{:S(2)}) copy-start(f32[8,32,128]{2,1,0:T(8,128)} %param.8) | copy-start | bytes 393220
  83.0 8.6 %copy-start.9 = (f32[5,8,32,128]{3,1,2,0:T(8,128)S(1)}, f32[5,8,32,128]{3,1,2,0:T(8,128)}, u32[]{:S(2)}) copy-start(f32[5,8,32,128]{3,1,2,0:T(8,128)} %copy-done.8) | copy-start | bytes 1966084
  83.0 17.4 %all-to-all-start.2 = ((f32[16,1,10240]{2,1,0:T(1,128)}), f32[16,1,10240]{2,1,0:T(1,128)S(1)}, u32[]{:S(2)}, u32[]{:S(2)}) async-start(f32[16,1,10240]{2,1,0:T(1,128)} %reshape.36), calls=%async_computation.2 | async-start | bytes 1310720 | tf_op jit(solution)/shard_map/all_to_all | solution.py:145
  124.5 10.3 %copy-start.13 = (f32[8,32,128]{2,0,1:T(8,128)S(1)}, f32[8,32,128]{2,0,1:T(8,128)}, u32[]{:S(2)}) copy-start(f32[8,32,128]{2,0,1:T(8,128)} %copy-done.12) | copy-start | bytes 393220
  124.5 10.3 %copy-start.20 = (f32[5,8,32,128]{3,1,2,0:T(8,128)S(1)}, f32[5,8,32,128]{3,1,2,0:T(8,128)}, u32[]{:S(2)}) copy-start(f32[5,8,32,128]{3,1,2,0:T(8,128)} %bitcast_dynamic-update-slice_fusion.4) | copy-start | bytes 1966084
  124.5 18.0 %copy-start.1 = (f32[8,32,128]{2,0,1:T(8,128)S(1)}, f32[8,32,128]{2,0,1:T(8,128)}, u32[]{:S(2)}) copy-start(f32[8,32,128]{2,0,1:T(8,128)} %copy-done) | copy-start | bytes 393220
  124.6 18.0 %copy-start.5 = (f32[8,32,128]{2,0,1:T(8,128)S(1)}, f32[8,32,128]{2,0,1:T(8,128)}, u32[]{:S(2)}) copy-start(f32[8,32,128]{2,0,1:T(8,128)} %copy-done.4) | copy-start | bytes 393220
  124.6 18.0 %copy-start.7 = (f32[4,8,32,128]{3,1,2,0:T(8,128)S(1)}, f32[4,8,32,128]{3,1,2,0:T(8,128)}, u32[]{:S(2)}) copy-start(f32[4,8,32,128]{3,1,2,0:T(8,128)} %fusion.98) | copy-start | bytes 1572868
  124.6 18.0 %copy-start.15 = (f32[8,32,128]{2,0,1:T(8,128)S(1)}, f32[8,32,128]{2,0,1:T(8,128)}, u32[]{:S(2)}) copy-start(f32[8,32,128]{2,0,1:T(8,128)} %copy-done.14) | copy-start | bytes 393220
  124.6 18.0 %copy-start.17 = (f32[8,32,128]{2,1,0:T(8,128)S(1)}, f32[8,32,128]{2,1,0:T(8,128)}, u32[]{:S(2)}) copy-start(f32[8,32,128]{2,1,0:T(8,128)} %param.8) | copy-start | bytes 393220
  128.1 14.8 %copy-start.24 = (f32[128,128,1,1]{1,0,3,2:T(8,128)S(1)}, f32[128,128,1,1]{1,0,3,2:T(8,128)}, u32[]{:S(2)}) copy-start(f32[128,128,1,1]{1,0,3,2:T(8,128)} %constant.34) | copy-start | bytes 196612
  128.1 24.8 %all-to-all-start.3 = ((f32[16,1,10240]{2,1,0:T(1,128)}), f32[16,1,10240]{2,1,0:T(1,128)S(1)}, u32[]{:S(2)}, u32[]{:S(2)}) async-start(f32[16,1,10240]{2,1,0:T(1,128)} %reshape.38), calls=%async_computation.3 | async-start | bytes 1310720 | tf_op jit(solution)/shard_map/all_to_all | solution.py:151
  134.9 27.6 %collective-permute-start.2 = (f32[5,4,32,128]{3,1,2,0:T(4,128)}, f32[5,4,32,128]{3,1,2,0:T(4,128)}, u32[]{:S(2)}, u32[]{:S(2)}) collective-permute-start(f32[5,4,32,128]{3,1,2,0:T(4,128)} %get-tuple-element.24), channel_id=1, source_target_pairs={{0,16},{16,32},{32,48},{48,64},{64,80},{80,96},{96,112},{112,128},... | collective-permute-start | bytes 983048 | tf_op jit(solution)/shard_map/ppermute | solution.py:28
  136.8 25.7 %collective-permute-start.3 = (f32[5,4,32,128]{3,1,2,0:T(4,128)}, f32[5,4,32,128]{3,1,2,0:T(4,128)}, u32[]{:S(2)}, u32[]{:S(2)}) collective-permute-start(f32[5,4,32,128]{3,1,2,0:T(4,128)} %get-tuple-element.25), channel_id=1, source_target_pairs={{16,0},{32,16},{48,32},{64,48},{80,64},{96,80},{112,96},{128,112},... | collective-permute-start | bytes 983048 | tf_op jit(solution)/shard_map/ppermute | solution.py:29
  (10 other events, 21.3 us)
